TPU v7x, 512 devices: a whole 4x4x16 slice. The times are simulated.
512 devices in a mesh: tm: 16 (over z), tensor: 32 (over y, x, core).
Axes of the slice: x: 4, y: 4, z: 16, core: 2. Of those that a mesh axis runs over, the one named last changes fastest.
Arguments:
- integrals: bfloat16 [1024, 8, 4096], P('tensor'), may hold values from -0.75 to 0.75
- pair_lists: int32 [16, 8], replicated, may hold values from 0 to 31, as said below
- occ_density: bfloat16 [16, 32, 64, 64], P('tm', 'tensor'), may hold values from -0.75 to 0.75
- virt_density: bfloat16 [16, 32, 64, 64], P('tm', 'tensor'), may hold values from -0.75 to 0.75
- cosine_weights: float32 [16, 16], replicated, may hold values from -1.5 to 1.5
- coulomb_blocks: float32 [16, 64, 64], replicated, may hold values from -0.75 to 0.75
Outputs:
- screened: float32 [16, 1024, 1024], P('tm', 'tensor')
Inputs may be any that keep to these rules, and one draw needn't show every extreme that they name: `pair_lists`: row p names the 8 pair blocks listed with aux block p, all different, in ascending order. Every pair block is named in 1 to 6 rows, and some pair block in exactly 6 rows.
All inputs are finite; a program needn't handle non-finite values.
Results may differ from a plain program's by a relative error of at most 0.01.
Values may be sent and summed in bfloat16 or wider, within the bound.
A program may use at most 64 MiB of HBM per device.

v0:
```python
import jax
import jax.numpy as jnp
from jax import lax
from jax.sharding import PartitionSpec as P

MOST = 6


def listed_blocks(pair_lists, pair_index):
    block_count = pair_lists.shape[0]
    member = jnp.any(pair_lists == pair_index, axis=1)
    positions = jnp.cumsum(member.astype(jnp.int32)) - 1
    slot_ids = jnp.arange(MOST, dtype=jnp.int32)
    matches = member[None, :] & (positions[None, :] == slot_ids[:, None])
    labels = jnp.arange(block_count, dtype=jnp.int32)
    located = jnp.sum(jnp.where(matches, labels[None, :], 0), axis=1)
    return jnp.where(jnp.any(matches, axis=1), located, block_count)


def density_product(row_data, occupied, virtual):
    row_count = row_data.shape[0]
    orbital_width = occupied.shape[0]
    half_done = jnp.dot(
        row_data.reshape(row_count * orbital_width, orbital_width),
        virtual,
        preferred_element_type=jnp.float32,
    )
    half_done = half_done.astype(jnp.bfloat16).reshape(row_count, orbital_width, orbital_width)
    contracted = jnp.einsum("rms,ml->rls", half_done, occupied, preferred_element_type=jnp.float32)
    return contracted.astype(jnp.bfloat16).reshape(row_count, orbital_width * orbital_width)


def pack_rows(local_rows, first_row, pair_lists, pair_count, block_rows):
    row_count = local_rows.shape[0]
    row_ids = first_row + jnp.arange(row_count, dtype=jnp.int32)
    targets = pair_lists[row_ids // block_rows]
    places = jnp.broadcast_to(jnp.arange(row_count, dtype=jnp.int32)[:, None], targets.shape)
    zero_buffer = jnp.zeros((pair_count, row_count, local_rows.shape[2]), local_rows.dtype)
    filled = zero_buffer.at[targets, places].set(local_rows)
    return filled.reshape(pair_count * row_count, local_rows.shape[2])


def per_device(integrals, pair_lists, occ_density, virt_density, cosine_weights, coulomb_blocks):
    tensor_size = lax.axis_size("tensor")
    owner_pair = lax.axis_index("tensor")
    local_count = integrals.shape[0]
    slab_rows = local_count * tensor_size
    block_count = coulomb_blocks.shape[0]
    block_rows = coulomb_blocks.shape[1]
    occupied = occ_density[0, 0]
    virtual = virt_density[0, 0]
    chosen = listed_blocks(pair_lists, owner_pair)
    wanted = (
        chosen[:, None] * block_rows + jnp.arange(block_rows, dtype=jnp.int32)[None, :]
    ).reshape(-1)
    outgoing = pack_rows(integrals, owner_pair * local_count, pair_lists, tensor_size, block_rows)
    arrived = lax.all_to_all(outgoing, "tensor", split_axis=0, concat_axis=0, tiled=True)
    tile_rows = jnp.take(arrived, wanted, axis=0, mode="fill", fill_value=0)
    weighted = density_product(tile_rows, occupied, virtual)
    gram_block = lax.dot_general(
        weighted, tile_rows, (((1,), (1,)), ((), ())), preferred_element_type=jnp.float32
    )
    most_count = chosen.shape[0]
    squares = gram_block.reshape(most_count, block_rows, most_count, block_rows).transpose(
        0, 2, 1, 3
    )
    partial_value = jnp.zeros((block_count, block_rows, block_count, block_rows), jnp.float32)
    partial_value = (
        partial_value.at[chosen[:, None], :, chosen[None, :], :]
        .set(squares, mode="drop")
        .reshape(slab_rows, slab_rows)
    )
    chi_rows = lax.psum_scatter(
        partial_value.astype(jnp.bfloat16), "tensor", scatter_dimension=0, tiled=True
    ).astype(jnp.float32)
    spread = jnp.einsum(
        "ft,trc->frc",
        cosine_weights,
        lax.all_to_all(
            chi_rows[None].astype(jnp.bfloat16), "tm", split_axis=2, concat_axis=0, tiled=True
        ).astype(jnp.float32),
        precision=lax.Precision.HIGHEST,
    )
    freq_rows = lax.all_to_all(
        spread.astype(jnp.bfloat16), "tm", split_axis=0, concat_axis=2, tiled=True
    ).astype(spread.dtype)
    shaped = freq_rows.reshape(1, local_count, block_count, block_rows)
    screened = jnp.einsum("frpa,pab->frpb", shaped, coulomb_blocks, precision=lax.Precision.HIGHEST)
    return screened.reshape(1, local_count, slab_rows)


def solution(mesh):
    in_specs = (
        P("tensor", None, None),
        P(),
        P("tm", "tensor", None, None),
        P("tm", "tensor", None, None),
        P(),
        P(),
    )
    out_specs = P("tm", "tensor", None)
    return jax.shard_map(
        per_device, mesh=mesh, in_specs=in_specs, out_specs=out_specs, check_vma=False
    )
```

profile of v0, /device:TPU:6, one launch (start us, length us, event | category | flops | bytes accessed | tf_op | source)
XLA Modules:
  0.0 452.2 jit_solution(2660522276019764714)
XLA Ops:
  6.6 0.8 copy.31
  7.4 0.6 gather_fusion
  8.1 4.3 broadcast_in_dim.71
  12.3 65.3 %scatter_fusion = bf16[32,32,4096]{2,1,0:T(8,128)(2,1)} fusion(bf16[32,32,4096]{2,1,0:T(8,128)(2,1)} %broadcast_in_dim.71, s32[256]{0:T(256)S(1)} %reshape.287, bf16[256,4096]{1,0:T(8,128)(2,1)S(1)} %bitcast.70), kind=kCustom, calls=%fused_computation.2 | custom fusion | bytes 6293504 | tf_op jit(solution)/shard_map/scatter | solution.py:39
  77.7 10.3 %all-to-all-start = ((bf16[32,32,4096]{2,1,0:T(8,128)(2,1)}), bf16[32,32,4096]{2,1,0:T(8,128)(2,1)}, u32[]{:S(2)}, u32[]{:S(2)}) async-start(bf16[32,32,4096]{2,1,0:T(8,128)(2,1)} %scatter_fusion), calls=%async_computation | async-start | bytes 16777216 | tf_op jit(solution)/shard_map/all_to_all | solution.py:57
  89.3 97.5 %all-to-all-done = bf16[32,32,4096]{2,1,0:T(8,128)(2,1)} async-done(((bf16[32,32,4096]{2,1,0:T(8,128)(2,1)}), bf16[32,32,4096]{2,1,0:T(8,128)(2,1)}, u32[]{:S(2)}, u32[]{:S(2)}) %all-to-all-start) | async-done | bytes 8388640 | tf_op jit(solution)/shard_map/all_to_all | solution.py:57
  186.8 12.7 %gather_fusion.1 = bf16[384,4096]{1,0:T(8,128)(2,1)} fusion(bf16[1024,4096]{1,0:T(8,128)(2,1)} %bitcast.4, s32[1024]{0:T(1024)S(1)} %pad_clamp_fusion), kind=kCustom, calls=%fused_computation.1 | custom fusion | bytes 6292992 | tf_op jit(solution)/shard_map/jit(_take)/gather | solution.py:58
  199.5 4.4 broadcast_select_fusion.1
  203.9 9.7 %select_n.125 = bf16[24576,64]{1,0:T(8,128)(2,1)} reshape(bf16[384,4096]{1,0:T(8,128)(2,1)} %get-tuple-element.7) | data formatting | bytes 6291456 | tf_op jit(solution)/shard_map/jit(_take)/select_n | solution.py:58
  213.6 6.8 %convolution_convert_fusion = bf16[24576,64]{0,1:T(8,128)(2,1)} fusion(bf16[24576,64]{1,0:T(8,128)(2,1)} %select_n.125, bf16[1,1,64,64]{3,2,1,0:T(8,128)(2,1)S(1)} %copy-done.2), kind=kOutput, calls=%fused_computation.4 | convolution fusion | flops 202899456 | bytes 6299648 | tf_op jit(solution)/shard_map/dot_general | solution.py:23
  220.4 9.7 %reshape.267 = bf16[384,64,64]{1,0,2:T(8,128)(2,1)} reshape(bf16[24576,64]{0,1:T(8,128)(2,1)} %convolution_convert_fusion) | data formatting | bytes 6291456 | tf_op jit(solution)/shard_map/reshape | solution.py:28
  230.1 6.8 %convert_bitcast_fusion = bf16[384,64,64]{0,1,2:T(8,128)(2,1)} fusion(bf16[384,64,64]{1,0,2:T(8,128)(2,1)} %reshape.267, bf16[1,1,64,64]{3,2,1,0:T(8,128)(2,1)S(1)} %copy-done.3), kind=kOutput, calls=%fused_computation.7 | convolution fusion | flops 202899456 | bytes 6299648 | tf_op jit(solution)/shard_map/rms,ml->rls/dot_general | solution.py:29
  236.8 12.3 %copy.34 = bf16[384,64,64]{2,1,0:T(8,128)(2,1)} copy(bf16[384,64,64]{0,1,2:T(8,128)(2,1)} %convert_bitcast_fusion) | data formatting | bytes 6291456 | tf_op jit(solution)/shard_map/convert_element_type | solution.py:30
  249.1 9.1 %reshape.300 = bf16[6,64,4096,1]{2,1,0,3:T(8,128)(2,1)} reshape(bf16[384,64,64]{2,1,0:T(8,128)(2,1)} %copy.34) | data formatting | bytes 6291456 | tf_op jit(solution)/shard_map/dot_general | solution.py:60
  258.3 5.5 %fusion = f32[6,64,6,64]{3,1,2,0:T(8,128)S(1)} fusion(bf16[6,64,4096,1]{2,1,0,3:T(8,128)(2,1)} %bitcast.69, bf16[6,64,4096,1]{2,1,0,3:T(8,128)(2,1)} %reshape.300), kind=kOutput, calls=%fused_computation.5 | convolution fusion | flops 1207959552 | bytes 6881280 | tf_op jit(solution)/shard_map/dot_general | solution.py:60
  263.7 4.3 broadcast_in_dim.64
  268.0 6.6 %scatter_fusion.1 = f32[16,64,16,64]{3,1,2,0:T(8,128)} fusion(f32[16,64,16,64]{3,1,2,0:T(8,128)} %broadcast_in_dim.64, s32[36]{0:T(128)S(1)} %reshape.293, f32[36,64,64]{2,1,0:T(8,128)S(1)} %bitcast.73), kind=kCustom, calls=%fused_computation.3 | custom fusion | bytes 1769760 | tf_op jit(solution)/shard_map/scatter | solution.py:70
  274.6 4.5 convert_element_type.48
  279.1 5.5 %copy.35 = bf16[16,64,16,64]{3,2,1,0:T(8,128)(2,1)} copy(bf16[16,64,16,64]{3,1,2,0:T(8,128)(2,1)S(1)} %convert_element_type.48) | data formatting | bytes 4194304 | tf_op jit(solution)/shard_map/convert_element_type | solution.py:74
  284.6 6.5 %convert_element_type.49 = bf16[1024,1024]{1,0:T(8,128)(2,1)} reshape(bf16[16,64,16,64]{3,2,1,0:T(8,128)(2,1)} %copy.35) | data formatting | bytes 4194304 | tf_op jit(solution)/shard_map/convert_element_type | solution.py:74
  291.1 106.8 %reduce-scatter.2.cloned.1.call-done = bf16[32,1024]{1,0:T(8,128)(2,1)} async-done(((bf16[1024,1024]{1,0:T(8,128)(2,1)}), bf16[32,1024]{1,0:T(8,128)(2,1)}) %reduce-scatter.2.cloned.1.call-update) | async-done | bytes 65552 | tf_op jit(solution)/shard_map/reduce_scatter | solution.py:73
  398.0 1.1 copy.36
  399.1 0.5 broadcast.351
  399.6 2.3 reduce.4
  401.9 0.3 reshape.306
  402.2 25.0 %all_to_all.42 = bf16[16,2,1024]{2,1,0:T(2,128)(2,1)S(1)} all-to-all(bf16[16,2,1024]{2,1,0:T(2,128)(2,1)S(1)} %reshape.306), channel_id=1, replica_groups=mesh['tm'=16,'tensor'=32] {'tm'}, dimensions={0} | all-to-all | bytes 131072 | tf_op jit(solution)/shard_map/all_to_all | solution.py:79
  427.1 0.3 reshape.307
  427.5 0.3 copy.37
  427.9 0.2 fusion.2
  428.4 15.5 %all_to_all.43 = bf16[16,2,1024]{2,1,0:T(2,128)(2,1)S(1)} all-to-all(bf16[16,2,1024]{2,1,0:T(2,128)(2,1)S(1)} %reshape.308), channel_id=1, replica_groups=mesh['tm'=16,'tensor'=32] {'tm'}, dimensions={0} | all-to-all | bytes 131072 | tf_op jit(solution)/shard_map/all_to_all | solution.py:84
  444.1 0.4 convolution_bitcast_fusion
  444.6 0.8 reshape.269
  (43 shorter events, 2.1 us)
Async XLA Ops:
  6.5 437.5 %copy-start = (f32[16,64,64]{2,1,0:T(8,128)S(1)}, f32[16,64,64]{2,1,0:T(8,128)}, u32[]{:S(2)}) copy-start(f32[16,64,64]{2,1,0:T(8,128)} %param.11) | copy-start | bytes 786436
  8.1 4.3 copy-start.1
  77.7 10.5 %copy-start.4 = (s32[16,8]{0,1:T(8,128)S(1)}, s32[16,8]{0,1:T(8,128)}, u32[]{:S(2)}) copy-start(s32[16,8]{0,1:T(8,128)} %param.7) | copy-start | bytes 1540
  77.7 109.1 %all-to-all-start = ((bf16[32,32,4096]{2,1,0:T(8,128)(2,1)}), bf16[32,32,4096]{2,1,0:T(8,128)(2,1)}, u32[]{:S(2)}, u32[]{:S(2)}) async-start(bf16[32,32,4096]{2,1,0:T(8,128)(2,1)} %scatter_fusion), calls=%async_computation | async-start | bytes 16777216 | tf_op jit(solution)/shard_map/all_to_all | solution.py:57
  88.0 310.0 %reduce-scatter.2.cloned.1.call-start = ((), (), s32[]{:S(2)}) async-start(), calls=%async_computation.4 | async-start | bytes 2162688 | tf_op jit(solution)/shard_map/reduce_scatter | solution.py:73
  203.9 9.7 %copy-start.2 = (bf16[1,1,64,64]{3,2,1,0:T(8,128)(2,1)S(1)}, bf16[1,1,64,64]{3,2,1,0:T(8,128)(2,1)}, u32[]{:S(2)}) copy-start(bf16[1,1,64,64]{3,2,1,0:T(8,128)(2,1)} %param.9) | copy-start | bytes 24580
  220.4 9.7 %copy-start.3 = (bf16[1,1,64,64]{3,2,1,0:T(8,128)(2,1)S(1)}, bf16[1,1,64,64]{3,2,1,0:T(8,128)(2,1)}, u32[]{:S(2)}) copy-start(bf16[1,1,64,64]{3,2,1,0:T(8,128)(2,1)} %param.8) | copy-start | bytes 24580
  291.1 136.8 %copy-start.5 = (f32[16,16]{1,0:T(8,128)S(1)}, f32[16,16]{1,0:T(8,128)}, u32[]{:S(2)}) copy-start(f32[16,16]{1,0:T(8,128)} %param.10) | copy-start | bytes 3076
Sparse Core Ops, SparseCore 0:
  291.3 106.6 reduce-scatter.1
where the time goes:
time: 455 us; the launch traced here: 452 us
  waiting for transfers between devices  204 us (45%)
  local copies, waits for them, and re-layouts  152 us (33%)
  blocking collectives  40.5 us (9%)
  matrix products  19.6 us (4%)
  between operations  13.6 us (3%)
  other arithmetic  11.9 us (3%)
  starting transfers between devices  10.5 us (2%)
    reduce_scatter x1, waiting for transfers between devices, per_device(): lax.psum_scatter(partial_value.astype(jnp.bfloat16), 'tensor', scatter_di...  107 us
    all_to_all x1, waiting for transfers between devices, per_device(): lax.all_to_all(outgoing, 'tensor', split_axis=0, concat_axis=0, tiled=True)  97.5 us
    scatter x1, local copies, waits for them, and re-layouts, pack_rows(): filled = zero_buffer.at[targets, places].set(local_rows)  65.3 us
    all_to_all x1, blocking collectives, per_device(): lax.all_to_all(chi_rows[None].astype(jnp.bfloat16), 'tm', split_axis=2, c...  25 us
    all_to_all x1, blocking collectives, per_device(): lax.all_to_all(spread.astype(jnp.bfloat16), 'tm', split_axis=0, concat_ax...  15.5 us
    gather x1, local copies, waits for them, and re-layouts, per_device(): tile_rows = jnp.take(arrived, wanted, axis=0, mode='fill', fill_value=0)  12.7 us
    convert_element_type x1, local copies, waits for them, and re-layouts, density_product(): contracted.astype(jnp.bfloat16)  12.3 us
    convert_element_type x2, local copies, waits for them, and re-layouts, per_device(): partial_value.astype(jnp.bfloat16)  12 us
  transfers between devices with their start and end apart: 2, of which 2 were waited for; matrix products, arithmetic and copies ran while one was open for 0% of the time, Pallas kernels for 0%

commit v1 on v0

v1 whole, which is shorter than its diff:
```python
import jax
import jax.numpy as jnp
from jax import lax
from jax.experimental import pallas as pl
from jax.experimental.pallas import tpu as pltpu
from jax.sharding import PartitionSpec as P

MESH = pl.DeviceIdType.MESH
MOST = 6
PB = 16
ORB = 64
ROWS = 32
PAIRS = 32
TIMES = 16
WIDTH = 256
SLOTS = MOST * 64
NT = (((1,), (1,)), ((), ()))
TN = (((0,), (0,)), ((), ()))


def tables(pair_lists, me, listed):
    ks = jnp.concatenate([me[None], listed])
    member = jnp.any(pair_lists[None] == ks[:, None, None], axis=2)
    before = jnp.arange(PB)[None, :] < jnp.arange(PB)[:, None]
    rank = jnp.sum((member[:, None, :] & before[None]).astype(jnp.int32), axis=2)
    labels = jnp.arange(PB, dtype=jnp.int32)
    hit = member[0][None, :] & (rank[0][None, :] == jnp.arange(MOST)[:, None])
    chosen = PB - jnp.sum(jnp.where(hit, PB - labels[None, :], 0), axis=1)
    slot_of = jnp.where(member[0], rank[0], 0)
    places = jnp.where(member[1:], listed[:, None] * MOST + rank[1:], PAIRS * MOST)
    return chosen.astype(jnp.int32), slot_of.astype(jnp.int32), places.astype(jnp.int32)


def iota(shape, axis):
    return lax.broadcasted_iota(jnp.int32, shape, axis)


def gather_kernel(chosen_ref, stage_ref, t_ref, got, comp, send1, recv1, sendz, recvz):
    z = lax.axis_index("tm")
    me = lax.axis_index("tensor")
    right, left = lax.rem(z + 1, TIMES), lax.rem(z + TIMES - 1, TIMES)

    barrier = pltpu.get_barrier_semaphore()

    def greet(i, carry):
        pl.semaphore_signal(
            barrier, inc=1, device_id={"tensor": lax.rem(me + i, PAIRS)}, device_id_type=MESH
        )
        return carry

    lax.fori_loop(1, PAIRS, greet, 0)
    for side in (left, right):
        pl.semaphore_signal(barrier, inc=1, device_id={"tm": side}, device_id_type=MESH)
    pl.semaphore_wait(barrier, PAIRS + 1)

    block = lax.div(me, 2)
    first = pl.multiple_of(lax.rem(me, 2) * ROWS, ROWS)

    def exchange(i):
        peer = lax.rem(me + i, PAIRS)
        return pltpu.make_async_remote_copy(
            src_ref=stage_ref.at[peer],
            dst_ref=got.at[block, pl.ds(first, ROWS)],
            send_sem=send1.at[i],
            recv_sem=recv1.at[i],
            device_id={"tensor": peer},
            device_id_type=MESH,
        )

    def start(i, carry):
        exchange(i).start()
        return carry

    lax.fori_loop(1, PAIRS, start, 0)
    got[PB] = jnp.zeros((64, WIDTH), jnp.bfloat16)
    got[block, pl.ds(first, ROWS)] = stage_ref[me]
    unit = (iota((WIDTH, WIDTH), 0) == iota((WIDTH, WIDTH), 1)).astype(jnp.float32)
    unit = unit.astype(jnp.bfloat16)

    def finish(i, carry):
        exchange(i).wait()
        return carry

    lax.fori_loop(1, PAIRS, finish, 0)
    for j in range(MOST):
        comp[64 * j : 64 * j + 64] = got[chosen_ref[j]]
    own = lax.dot_general(unit, comp[...], NT, preferred_element_type=jnp.float32)
    t_ref[pl.ds(4 * z, 4)] = own.astype(jnp.bfloat16).reshape(4, ORB, SLOTS)

    def hop(way, step, half):
        owner = lax.rem(z + (TIMES - (step - 1) if way == 0 else step - 1), TIMES)
        piece = t_ref.at[pl.ds(4 * owner + 2 * half, 2)]
        return pltpu.make_async_remote_copy(
            src_ref=piece,
            dst_ref=piece,
            send_sem=sendz.at[way, step - 1, half],
            recv_sem=recvz.at[way, step - 1, half],
            device_id={"tm": right if way == 0 else left},
            device_id_type=MESH,
        )

    last = TIMES // 2
    for step in range(1, last + 1):
        for half in range(2):
            for way in range(2):
                if step > 1:
                    hop(way, step - 1, half).wait_recv()
                if step < last or half == way:
                    hop(way, step, half).start()
    for way in range(2):
        hop(way, last, way).wait_recv()
    for step in range(1, last + 1):
        for half in range(2):
            for way in range(2):
                if step < last or half == way:
                    hop(way, step, half).wait_send()


def term_kernel(
    chosen_ref, slot_ref, t_ref, occ_ref, virt_ref, left_ref, right_ref, out_ref,
    ko, kv, half, gram, lead, trail, folded,
):
    big, small = ORB * 16, ORB * 4
    pick = (lax.div(iota((big, ORB), 0), 16) == iota((big, ORB), 1)).astype(jnp.float32)
    pick = pick.astype(jnp.bfloat16)
    rows = lax.dot_general(pick, occ_ref[...], NT, preferred_element_type=jnp.float32)
    full = lax.dot_general(
        rows.astype(jnp.bfloat16), pick, NT, preferred_element_type=jnp.float32
    )
    same = lax.rem(iota((big, big), 0), 16) == lax.rem(iota((big, big), 1), 16)
    ko[...] = jnp.where(same, full, 0.0).astype(jnp.bfloat16)
    pick = (lax.rem(iota((small, ORB), 0), ORB) == iota((small, ORB), 1)).astype(jnp.float32)
    pick = pick.astype(jnp.bfloat16)
    rows = lax.dot_general(pick, virt_ref[...], NT, preferred_element_type=jnp.float32)
    full = lax.dot_general(
        rows.astype(jnp.bfloat16), pick, NT, preferred_element_type=jnp.float32
    )
    same = lax.div(iota((small, small), 0), ORB) == lax.div(iota((small, small), 1), ORB)
    kv[...] = jnp.where(same, full, 0.0).astype(jnp.bfloat16)

    lead[...] = jnp.zeros_like(lead)
    trail[...] = jnp.zeros_like(trail)
    for j in range(MOST):
        block = jnp.minimum(chosen_ref[j], PB - 1)
        lead[64 * j : 64 * j + 64, 128 * j : 128 * j + 128] = left_ref[block]
        trail[64 * j : 64 * j + 64, 128 * j : 128 * j + 128] = right_ref[block]

    def occupied(g, carry):
        nus = pl.ds(pl.multiple_of(g * 16, 16), 16)
        part = jnp.dot(
            ko[...], t_ref[:, nus, :].reshape(big, SLOTS), preferred_element_type=jnp.float32
        )
        half[:, nus, :] = part.astype(jnp.bfloat16).reshape(ORB, 16, SLOTS)
        return carry

    lax.fori_loop(0, 4, occupied, 0)
    gram[...] = jnp.zeros_like(gram)

    def virtual(b, carry):
        lams = pl.ds(b * 4, 4)
        mixed = jnp.dot(
            kv[...], half[lams].reshape(small, SLOTS), preferred_element_type=jnp.float32
        )
        gram[...] += lax.dot_general(
            mixed.astype(jnp.bfloat16), t_ref[lams].reshape(small, SLOTS), TN,
            preferred_element_type=jnp.float32,
        )
        return carry

    lax.fori_loop(0, 16, virtual, 0)
    term = gram[...].astype(jnp.bfloat16)
    upper = jnp.dot(term, lead[...], preferred_element_type=jnp.float32)
    lower = jnp.dot(term, trail[...], preferred_element_type=jnp.float32)
    for b in range(2 * MOST):
        both = upper[32 * b : 32 * b + 16] + lower[32 * b + 16 : 32 * b + 32]
        both = both.astype(jnp.bfloat16)
        for j in range(MOST):
            folded[b, j] = both[:, 128 * j : 128 * j + 128]
    for d in range(PAIRS):
        out_ref[d] = folded[slot_ref[d // 2] * 2 + d % 2]


def merge_kernel(
    place_ref, cos_ref, term_ref, out_ref, got, chi, times, spread, freqs,
    send1, recv1, send2, recv2, send3, recv3,
):
    z = lax.axis_index("tm")
    me = lax.axis_index("tensor")
    barrier = pltpu.get_barrier_semaphore()

    def greet(i, carry):
        pl.semaphore_signal(
            barrier, inc=1, device_id={"tensor": lax.rem(me + i, PAIRS)}, device_id_type=MESH
        )
        return carry

    def greet_far(i, carry):
        pl.semaphore_signal(
            barrier, inc=1, device_id={"tm": lax.rem(z + i, TIMES)}, device_id_type=MESH
        )
        return carry

    lax.fori_loop(1, TIMES, greet_far, 0)
    lax.fori_loop(1, PAIRS, greet, 0)
    pl.semaphore_wait(barrier, PAIRS + TIMES - 2)

    def exchange(i):
        peer = lax.rem(me + i, PAIRS)
        return pltpu.make_async_remote_copy(
            src_ref=term_ref.at[peer],
            dst_ref=got.at[pl.ds(me * MOST, MOST)],
            send_sem=send1.at[i],
            recv_sem=recv1.at[i],
            device_id={"tensor": peer},
            device_id_type=MESH,
        )

    def start(i, carry):
        exchange(i).start()
        return carry

    def finish(i, carry):
        exchange(i).wait()
        return carry

    lax.fori_loop(1, PAIRS, start, 0)
    got[PAIRS * MOST] = jnp.zeros((16, 128), jnp.bfloat16)
    got[pl.ds(me * MOST, MOST)] = term_ref[me]
    lax.fori_loop(1, PAIRS, finish, 0)

    for q in range(PB):
        total = got[place_ref[0, q]].astype(jnp.float32)
        for c in range(1, 8):
            total += got[place_ref[c, q]].astype(jnp.float32)
        chi[q] = total.astype(jnp.bfloat16)

    def trade(src, dst, send, recv):
        def one(i):
            peer = lax.rem(z + i, TIMES)
            return pltpu.make_async_remote_copy(
                src_ref=src.at[peer],
                dst_ref=dst.at[z],
                send_sem=send.at[i],
                recv_sem=recv.at[i],
                device_id={"tm": peer},
                device_id_type=MESH,
            )

        def begin(i, carry):
            one(i).start()
            return carry

        def end(i, carry):
            one(i).wait()
            return carry

        lax.fori_loop(1, TIMES, begin, 0)
        dst[z] = src[z]
        lax.fori_loop(1, TIMES, end, 0)

    trade(chi, times, send2, recv2)
    series = [times[t].astype(jnp.float32) for t in range(TIMES)]
    for f in range(TIMES):
        total = cos_ref[f, 0] * series[0]
        for t in range(1, TIMES):
            total += cos_ref[f, t] * series[t]
        spread[f] = total.astype(jnp.bfloat16)
    trade(spread, freqs, send3, recv3)

    low = iota((16, 128), 1) < 64
    for m in range(PB // 2):
        even = freqs[2 * m].astype(jnp.float32)
        odd = freqs[2 * m + 1].astype(jnp.float32)
        lanes = slice(128 * m, 128 * m + 128)
        out_ref[0, 0:16, lanes] = jnp.where(low, even, pltpu.roll(odd, 64, 1))
        out_ref[0, 16:32, lanes] = jnp.where(low, pltpu.roll(even, 64, 1), odd)


def per_device(integrals, pair_lists, occ_density, virt_density, cosine_weights, coulomb_blocks):
    z = lax.axis_index("tm")
    me = lax.axis_index("tensor")
    listed = lax.dynamic_index_in_dim(pair_lists, me // 2, 0, keepdims=False)
    chosen, slot_of, places = tables(pair_lists, me, listed)

    mine = lax.dynamic_slice_in_dim(integrals, z * WIDTH, WIDTH, axis=2).reshape(ROWS * 8, WIDTH)
    wide = (PAIRS, ROWS, ROWS, 8)
    route = (iota(wide, 1) == iota(wide, 2)) & (iota(wide, 0) == listed[None, None, None, :])
    stage = jnp.dot(
        route.reshape(PAIRS * ROWS, ROWS * 8).astype(jnp.bfloat16),
        mine,
        preferred_element_type=jnp.float32,
    )
    stage = stage.astype(jnp.bfloat16).reshape(PAIRS, ROWS, WIDTH)
    factor = coulomb_blocks.astype(jnp.bfloat16)
    left_factor = jnp.pad(factor, ((0, 0), (0, 0), (0, 64)))
    right_factor = jnp.pad(factor, ((0, 0), (0, 0), (64, 0)))

    smem = pl.BlockSpec(memory_space=pltpu.SMEM)
    vmem = pl.BlockSpec(memory_space=pltpu.VMEM)
    dma = pltpu.SemaphoreType.DMA
    tiles = pl.pallas_call(
        gather_kernel,
        out_shape=jax.ShapeDtypeStruct((ORB, ORB, SLOTS), jnp.bfloat16),
        in_specs=[smem, vmem],
        out_specs=vmem,
        scratch_shapes=[
            pltpu.VMEM((PB + 1, 64, WIDTH), jnp.bfloat16),
            pltpu.VMEM((SLOTS, WIDTH), jnp.bfloat16),
            dma((PAIRS,)),
            dma((PAIRS,)),
            dma((2, 8, 2)),
            dma((2, 8, 2)),
        ],
        compiler_params=pltpu.CompilerParams(collective_id=0, has_side_effects=True),
        name="gather_tiles",
    )(chosen, stage)
    terms = pl.pallas_call(
        term_kernel,
        out_shape=jax.ShapeDtypeStruct((PAIRS, MOST, 16, 128), jnp.bfloat16),
        in_specs=[smem, smem, vmem, vmem, vmem, vmem, vmem],
        out_specs=vmem,
        scratch_shapes=[
            pltpu.VMEM((1024, 1024), jnp.bfloat16),
            pltpu.VMEM((256, 256), jnp.bfloat16),
            pltpu.VMEM((ORB, ORB, SLOTS), jnp.bfloat16),
            pltpu.VMEM((SLOTS, SLOTS), jnp.float32),
            pltpu.VMEM((SLOTS, 2 * SLOTS), jnp.bfloat16),
            pltpu.VMEM((SLOTS, 2 * SLOTS), jnp.bfloat16),
            pltpu.VMEM((2 * MOST, MOST, 16, 128), jnp.bfloat16),
        ],
        name="pair_terms",
    )(
        chosen, slot_of, tiles, occ_density[0, 0], virt_density[0, 0], left_factor, right_factor
    )
    block = pltpu.VMEM((PB, 16, 128), jnp.bfloat16)
    return pl.pallas_call(
        merge_kernel,
        out_shape=jax.ShapeDtypeStruct((1, ROWS, PB * 64), jnp.float32),
        in_specs=[smem, smem, vmem],
        out_specs=vmem,
        scratch_shapes=[
            pltpu.VMEM((PAIRS * MOST + 1, 16, 128), jnp.bfloat16),
            block,
            block,
            block,
            block,
            dma((PAIRS,)),
            dma((PAIRS,)),
            dma((TIMES,)),
            dma((TIMES,)),
            dma((TIMES,)),
            dma((TIMES,)),
        ],
        compiler_params=pltpu.CompilerParams(collective_id=1, has_side_effects=True),
        name="merge_terms",
    )(places, cosine_weights, terms)


def solution(mesh):
    in_specs = (
        P("tensor", None, None),
        P(),
        P("tm", "tensor", None, None),
        P("tm", "tensor", None, None),
        P(),
        P(),
    )
    return jax.shard_map(
        per_device, mesh=mesh, in_specs=in_specs, out_specs=P("tm", "tensor", None), check_vma=False
    )
```

time: 455 us -> 127 us (0.28)
  waiting for transfers between devices: 204 us -> 0 us
  local copies, waits for them, and re-layouts: 152 us -> 3.89 us
  Pallas kernels: 0 us -> 117 us
  blocking collectives: 40.5 us -> 0 us
  matrix products: 19.6 us -> 1.25 us
  between operations: 13.6 us -> 0.07 us
  starting transfers between devices: 10.5 us -> 0 us
  other arithmetic: 11.9 us -> 4.1 us
    pallas_call x0 -> x3, Pallas kernels: none -> 117 us  [the longest x1 64.1 us: per_device(): pl.pallas_call(gather_kernel, out_shape=jax.ShapeDtypeStruct((ORB, ORB, S...]
    reduce_scatter x1 -> x0, waiting for transfers between devices: 107 us -> none  [per_device(): lax.psum_scatter(partial_value.astype(jnp.bfloat16), 'tensor', scatter_di...]
    all_to_all x1 -> x0, waiting for transfers between devices: 97.5 us -> none  [per_device(): lax.all_to_all(outgoing, 'tensor', split_axis=0, concat_axis=0, tiled=True)]
    scatter x2 -> x0, local copies, waits for them, and re-layouts: 71.9 us -> none  [the longest x1 65.3 us: pack_rows(): filled = zero_buffer.at[targets, places].set(local_rows)]
    all_to_all x2 -> x0, blocking collectives: 40.5 us -> none  [the longest x1 25 us: per_device(): lax.all_to_all(chi_rows[None].astype(jnp.bfloat16), 'tm', split_axis=2, c...]
    convert_element_type x6 -> x0, local copies, waits for them, and re-layouts: 25.5 us -> none  [the longest x1 12.3 us: density_product(): contracted.astype(jnp.bfloat16)]
    dot_general x5 -> x1, matrix products: 19.6 us -> 1.25 us  [per_device(): jnp.dot(route.reshape(PAIRS * ROWS, ROWS * 8).astype(jnp.bfloat16), mine,...]
    gather x2 -> x0, local copies, waits for them, and re-layouts: 13.3 us -> none  [the longest x1 12.7 us: per_device(): tile_rows = jnp.take(arrived, wanted, axis=0, mode='fill', fill_value=0)]
  transfers between devices with their start and end apart: 2 -> 0, of which waited for: 2 -> 0; matrix products, arithmetic and copies ran while one was open for 0% -> 0% of each run, Pallas kernels for 0% -> 0%
where the time goes in v1:
time: 127 us
  Pallas kernels  117 us (92%)
  other arithmetic  4.1 us (3%)
  local copies, waits for them, and re-layouts  3.89 us (3%)
    pallas_call x1, Pallas kernels, per_device(): pl.pallas_call(gather_kernel, out_shape=jax.ShapeDtypeStruct((ORB, ORB, S...  64.1 us
    pallas_call x1, Pallas kernels, per_device(): pl.pallas_call(merge_kernel, out_shape=jax.ShapeDtypeStruct((1, ROWS, PB...  35.5 us
    pallas_call x1, Pallas kernels, per_device(): pl.pallas_call(term_kernel, out_shape=jax.ShapeDtypeStruct((PAIRS, MOST,...  17.8 us

profile of v1, /device:TPU:6, one launch (start us, length us, event | category | flops | bytes accessed | tf_op | source)
XLA Modules:
  0.0 126.7 jit_solution(16377940681018572074)
XLA Ops:
  0.0 0.0 copy-start
  0.0 1.0 dynamic-slice_reduce_fusion
  1.0 0.1 pad_add_fusion
  1.1 0.8 compare_reduce_fusion
  1.9 0.2 convert_reduce_fusion
  2.2 0.6 broadcast_select_fusion.slot_ref
  2.8 0.7 fusion.9.place_ref
  3.4 0.1 select_reduce_fusion
  3.5 0.5 broadcast_subtract_fusion.chosen_ref
  4.1 0.1 eq.54
  4.2 0.1 iota.64
  4.2 0.1 iota.61
  4.3 0.1 iota.58
  4.4 1.1 convert_element_type.16
  5.5 1.0 fusion.12
  6.5 0.0 copy-done
  6.5 1.2 convolution_convert_fusion
  7.7 64.1 %gather_tiles.1.t_ref = bf16[64,64,384]{2,1,0:T(8,128)(2,1)} custom-call(s32[6]{0:T(128)} %broadcast_subtract_fusion.chosen_ref, bf16[32,32,256]{2,1,0:T(8,128)(2,1)} %bitcast.15), custom_call_target="tpu_custom_call" | custom-call | tf_op jit(solution)/shard_map/gather_tiles/pallas_call | solution.py:301
  71.8 17.8 %pair_terms.1.term_ref = bf16[32,6,16,128]{3,2,1,0:T(8,128)(2,1)} custom-call(s32[6]{0:T(128)} %broadcast_subtract_fusion.chosen_ref, s32[16]{0:T(128)} %broadcast_select_fusion.slot_ref, bf16[64,64,384]{2,1,0:T(8,128)(2,1)} %gather_tiles.1.t_ref, bf16[64,64]{1,0:T(8,128)(2,1)} %bitcast.16, bf16[64,64]{1,0:T(8,128)(2,1)} %bitcast.17, ...), custom_call_target="tpu_custom_call" | custom-call | tf_op jit(solution)/shard_map/pair_terms/pallas_call | solution.py:317
  89.6 35.5 %merge_terms.1 = f32[1,32,1024]{2,1,0:T(8,128)} custom-call(s32[8,16]{1,0:T(8,128)} %fusion.9.place_ref, f32[16,16]{1,0:T(8,128)} %cos_ref.1, bf16[32,6,16,128]{3,2,1,0:T(8,128)(2,1)} %pair_terms.1.term_ref), custom_call_target="tpu_custom_call" | custom-call | tf_op jit(solution)/shard_map/merge_terms/pallas_call | solution.py:336
  125.1 1.6 %copy.10 = f32[1,32,1024]{2,1,0:T(8,128)} copy(f32[1,32,1024]{2,1,0:T(8,128)} %merge_terms.1) | data formatting | bytes 262144
  (9 shorter events, 0.0 us)
Async XLA Ops:
  0.0 6.5 %copy-start = (bf16[32,8,4096]{2,1,0:T(8,128)(2,1)S(1)}, bf16[32,8,4096]{2,1,0:T(8,128)(2,1)}, u32[]{:S(2)}) copy-start(bf16[32,8,4096]{2,1,0:T(8,128)(2,1)} %param.6) | copy-start | bytes 6291460

commit v2 on v0

v2 whole, which is shorter than its diff:
```python
import jax
import jax.numpy as jnp
from jax import lax
from jax.experimental import pallas as pl
from jax.experimental.pallas import tpu as pltpu
from jax.sharding import PartitionSpec as P

MESH = pl.DeviceIdType.MESH
MOST = 6
PB = 16
CAPS = 8
ORB = 64
ROWS = 32
PAIRS = 32
TIMES = 16
WIDTH = 256
SLOTS = MOST * 64
STEPS = 6
CHUNKS = 2
NT = (((1,), (1,)), ((), ()))
TN = (((0,), (0,)), ((), ()))
ORDER = (0, 1, -1, 2, -2, 3, -3, 8, 4, -4, 7, 5, -5, -7, 6, -6)
PLACE = {distance: place for place, distance in enumerate(ORDER)}
DIRECT = (0, 8, 7, -7)


def iota(shape, axis):
    return lax.broadcasted_iota(jnp.int32, shape, axis)


def one_hot(mask):
    return mask.astype(jnp.float32).astype(jnp.bfloat16)


def mul(a, b, dims=None):
    if dims is None:
        return jnp.dot(a, b, preferred_element_type=jnp.float32)
    return lax.dot_general(a, b, dims, preferred_element_type=jnp.float32)


def low(x):
    return x.astype(jnp.bfloat16)


def kernel(
    lists_ref, cos_ref, rows_ref, factor_ref, occ_ref, virt_ref, out_ref,
    mine, route, stage, got0, got1, got2, got3, comp, tiles, factor, ko, kv, lead, trail, part, half, gram, folded,
    terms, inbox, chi, times, spread, freqs, places,
    load_sem, factor_sem, send1, recv1, sendz, recvz, send2, recv2, send3, recv3, send4, recv4,
):
    z = lax.axis_index("tm")
    me = lax.axis_index("tensor")
    got = (got0, got1, got2, got3)
    block = lax.div(me, 2)
    first = pl.multiple_of(lax.rem(me, 2) * ROWS, ROWS)

    def at(distance):
        return lax.rem(z + distance + TIMES, TIMES)

    def load(e):
        columns = pl.ds(pl.multiple_of(at(DIRECT[e]) * WIDTH, WIDTH), WIDTH)
        return pltpu.make_async_copy(rows_ref.at[:, columns], mine.at[e], load_sem.at[e])

    for e in range(len(DIRECT)):
        load(e).start()
    fetch = pltpu.make_async_copy(factor_ref, factor, factor_sem)
    fetch.start()

    barrier = pltpu.get_barrier_semaphore()

    def greet(i, carry):
        peer = lax.rem(me + i, PAIRS)
        pl.semaphore_signal(barrier, inc=1, device_id={"tensor": peer}, device_id_type=MESH)
        return carry

    for distance in (2, -2, 1, -1):
        pl.semaphore_signal(barrier, inc=1, device_id={"tm": at(distance)}, device_id_type=MESH)
    lax.fori_loop(1, PAIRS, greet, 0)

    column = lax.rem(iota((1, WIDTH), 1), CAPS)
    names = jnp.full((1, WIDTH), -1, jnp.int32)
    for c in range(CAPS):
        names = jnp.where(column == c, lists_ref[c, block], names)
    shape = (PAIRS * ROWS, WIDTH)
    listed = lax.div(iota(shape, 0), ROWS) == names
    same = lax.rem(iota(shape, 0), ROWS) == lax.div(iota(shape, 1), CAPS)
    route[...] = one_hot(listed & same)

    def pack(e):
        load(e).wait()
        stage[e] = low(mul(route[...], mine[e])).reshape(PAIRS, ROWS, WIDTH)

    pack(0)
    pl.semaphore_wait(barrier, PAIRS + 3)

    def exchange(e, i):
        peer = lax.rem(me + i, PAIRS)
        return pltpu.make_async_remote_copy(
            src_ref=stage.at[e, peer],
            dst_ref=got[e].at[block, pl.ds(first, ROWS)],
            send_sem=send1.at[e, i],
            recv_sem=recv1.at[e, i],
            device_id={"tensor": peer},
            device_id_type=MESH,
        )

    def send_rows(e):
        def start(i, carry):
            exchange(e, i).start()
            return carry

        lax.fori_loop(1, PAIRS, start, 0)

    send_rows(0)

    members, ranks, count = [], [], jnp.int32(0)
    for p in range(PB):
        named = lists_ref[0, p] == me
        for c in range(1, CAPS):
            named = named | (lists_ref[c, p] == me)
        members.append(named)
        ranks.append(count)
        count = count + named.astype(jnp.int32)
    chosen = []
    for j in range(MOST):
        found = jnp.int32(PB)
        for p in range(PB):
            found = jnp.where(members[p] & (ranks[p] == j), p, found)
        chosen.append(found)
    slot_of = [jnp.where(members[p], jnp.minimum(ranks[p], MOST - 1), 0) for p in range(PB)]

    for e in range(len(DIRECT)):
        got[e][PB] = jnp.zeros((64, WIDTH), jnp.bfloat16)
        if e:
            pack(e)
        got[e][block, pl.ds(first, ROWS)] = stage[e, me]
    unit = one_hot(iota((WIDTH, WIDTH), 0) == iota((WIDTH, WIDTH), 1))

    square = (ORB, ORB)
    held = lax.div(iota(square, 0), 4)
    owner = jnp.zeros(square, jnp.int32)
    for place, distance in enumerate(ORDER):
        owner = jnp.where(held == place, at(distance), owner)
    order = one_hot(iota(square, 1) == 4 * owner + lax.rem(iota(square, 0), 4))
    occ = low(mul(low(mul(order, occ_ref[...])), order, NT))
    big, small = ORB * 16, ORB * 4
    pick = one_hot(lax.div(iota((big, ORB), 0), 16) == iota((big, ORB), 1))
    full = mul(low(mul(pick, occ, NT)), pick, NT)
    same = lax.rem(iota((big, big), 0), 16) == lax.rem(iota((big, big), 1), 16)
    ko[...] = low(jnp.where(same, full, 0.0))
    pick = one_hot(lax.rem(iota((small, ORB), 0), ORB) == iota((small, ORB), 1))
    full = mul(low(mul(pick, virt_ref[...], NT)), pick, NT)
    same = lax.div(iota((small, small), 0), ORB) == lax.div(iota((small, small), 1), ORB)
    kv[...] = low(jnp.where(same, full, 0.0))

    def take_rows(e):
        def finish(i, carry):
            exchange(e, i).wait()
            return carry

        lax.fori_loop(1, PAIRS, finish, 0)
        for j in range(MOST):
            comp[64 * j : 64 * j + 64] = got[e][chosen[j]]
        place = PLACE[DIRECT[e]]
        tiles[4 * place : 4 * place + 4] = low(mul(unit, comp[...], NT)).reshape(4, ORB, SLOTS)

    def hop(way, step, chunk):
        sign = -1 if way == 0 else 1
        rows = 4 // CHUNKS
        source = 4 * PLACE[sign * (step - 1)] + rows * chunk
        target = 4 * PLACE[sign * step] + rows * chunk
        return pltpu.make_async_remote_copy(
            src_ref=tiles.at[source : source + rows],
            dst_ref=tiles.at[target : target + rows],
            send_sem=sendz.at[way, step - 1, chunk],
            recv_sem=recvz.at[way, step - 1, chunk],
            device_id={"tm": at(-sign)},
            device_id_type=MESH,
        )

    def contract(b, g0, g1):
        def one(g, carry):
            nus = pl.ds(pl.multiple_of(g * 16, 16), 16)
            x = tiles[16 * b : 16 * b + 16, nus, :].reshape(WIDTH, SLOTS)
            y = mul(ko[:, WIDTH * b : WIDTH * b + WIDTH], x)
            if b == 0:
                part[g] = y
            elif b < 3:
                part[g] += y
            else:
                half[:, nus, :] = low(part[g] + y).reshape(ORB, 16, SLOTS)
            return carry

        lax.fori_loop(g0, g1, one, 0)

    def factors():
        fetch.wait()
        lead[...] = jnp.zeros_like(lead)
        trail[...] = jnp.zeros_like(trail)
        wide = (ORB, 2 * ORB)
        ahead = one_hot(iota(wide, 0) == iota(wide, 1))
        behind = one_hot(iota(wide, 0) + ORB == iota(wide, 1))
        for j in range(MOST):
            value = low(factor[jnp.minimum(chosen[j], PB - 1)])
            lead[64 * j : 64 * j + 64, 128 * j : 128 * j + 128] = low(mul(value, ahead))
            trail[64 * j : 64 * j + 64, 128 * j : 128 * j + 128] = low(mul(value, behind))

    take_rows(0)
    under = {
        (1, 1): factors,
        (3, 1): lambda: contract(0, 0, 2),
        (4, 0): lambda: contract(0, 2, 4),
        (4, 1): lambda: take_rows(1),
        (5, 0): lambda: contract(1, 0, 2),
        (5, 1): lambda: contract(1, 2, 4),
        (6, 0): lambda: take_rows(2),
        (6, 1): lambda: contract(2, 0, 4),
    }
    for step in range(1, STEPS + 1):
        for chunk in range(CHUNKS):
            for way in range(2):
                if step > 1:
                    hop(way, step - 1, chunk).wait_recv()
                hop(way, step, chunk).start()
            if step == 1 and chunk == CHUNKS - 1:
                for e in range(1, len(DIRECT)):
                    send_rows(e)
            if (step, chunk) in under:
                under[step, chunk]()
    take_rows(3)
    for chunk in range(CHUNKS):
        for way in range(2):
            hop(way, STEPS, chunk).wait_recv()
    contract(3, 0, 4)
    gram[...] = jnp.zeros_like(gram)

    def virtual(b, carry):
        lams = pl.ds(b * 4, 4)
        mixed = low(mul(kv[...], half[lams].reshape(small, SLOTS)))
        gram[...] += mul(mixed, tiles[lams].reshape(small, SLOTS), TN)
        return carry

    lax.fori_loop(0, ORB // 4, virtual, 0)
    term = low(gram[...])
    upper, lower = mul(term, lead[...]), mul(term, trail[...])
    for b in range(2 * MOST):
        both = low(upper[32 * b : 32 * b + 16] + lower[32 * b + 16 : 32 * b + 32])
        for j in range(MOST):
            folded[b, j] = both[:, 128 * j : 128 * j + 128]
    for d in range(PAIRS):
        terms[d] = folded[slot_of[d // 2] * 2 + d % 2]

    def trade(axis, count, src, dst, send, recv):
        here = lax.axis_index(axis)

        def one(i):
            peer = lax.rem(here + i, count)
            return pltpu.make_async_remote_copy(
                src_ref=src.at[peer],
                dst_ref=dst.at[here],
                send_sem=send.at[i],
                recv_sem=recv.at[i],
                device_id={axis: peer},
                device_id_type=MESH,
            )

        def begin(i, carry):
            one(i).start()
            return carry

        def end(i, carry):
            one(i).wait()
            return carry

        lax.fori_loop(1, count, begin, 0)
        dst[here] = src[here]
        return lambda: lax.fori_loop(1, count, end, 0)

    arrive = trade("tensor", PAIRS, terms, inbox, send2, recv2)
    inbox[PAIRS, 0] = jnp.zeros((16, 128), jnp.bfloat16)

    def locate(c, carry):
        name = lists_ref[c, block]
        rank = jnp.int32(0)
        for q in range(PB):
            named = lists_ref[0, q] == name
            for other in range(1, CAPS):
                named = named | (lists_ref[other, q] == name)
            places[0, c * PB + q] = jnp.where(named, name, PAIRS)
            places[1, c * PB + q] = jnp.where(named, jnp.minimum(rank, MOST - 1), 0)
            rank = rank + named.astype(jnp.int32)
        return carry

    lax.fori_loop(0, CAPS, locate, 0)
    for step in range(1, STEPS + 1):
        for chunk in range(CHUNKS):
            for way in range(2):
                hop(way, step, chunk).wait_send()
    arrive()
    for q in range(PB):
        total = inbox[places[0, q], places[1, q]].astype(jnp.float32)
        for c in range(1, CAPS):
            spot = c * PB + q
            total += inbox[places[0, spot], places[1, spot]].astype(jnp.float32)
        chi[q] = low(total)

    trade("tm", TIMES, chi, times, send3, recv3)()
    series = [times[t].astype(jnp.float32) for t in range(TIMES)]
    for f in range(TIMES):
        total = cos_ref[f, 0] * series[0]
        for t in range(1, TIMES):
            total += cos_ref[f, t] * series[t]
        spread[f] = low(total)
    trade("tm", TIMES, spread, freqs, send4, recv4)()

    near = iota((16, 128), 1) < 64
    for m in range(PB // 2):
        even = freqs[2 * m].astype(jnp.float32)
        odd = freqs[2 * m + 1].astype(jnp.float32)
        lanes = slice(128 * m, 128 * m + 128)
        out_ref[0, 0:16, lanes] = jnp.where(near, even, pltpu.roll(odd, 64, 1))
        out_ref[0, 16:32, lanes] = jnp.where(near, pltpu.roll(even, 64, 1), odd)


def per_device(integrals, pair_lists, occ_density, virt_density, cosine_weights, coulomb_blocks):
    smem = pl.BlockSpec(memory_space=pltpu.SMEM)
    vmem = pl.BlockSpec(memory_space=pltpu.VMEM)
    hbm = pl.BlockSpec(memory_space=pl.ANY)
    dma = pltpu.SemaphoreType.DMA
    half = jnp.bfloat16
    direct = len(DIRECT)
    block = pltpu.VMEM((PB, 16, 128), half)
    arrived = pltpu.VMEM((PB + 1, 64, WIDTH), half)
    return pl.pallas_call(
        kernel,
        out_shape=jax.ShapeDtypeStruct((1, ROWS, PB * 64), jnp.float32),
        in_specs=[smem, smem, hbm, hbm, vmem, vmem],
        out_specs=vmem,
        scratch_shapes=[
            pltpu.VMEM((direct, ROWS * CAPS, WIDTH), half),
            pltpu.VMEM((PAIRS * ROWS, ROWS * CAPS), half),
            pltpu.VMEM((direct, PAIRS, ROWS, WIDTH), half),
            arrived,
            arrived,
            arrived,
            arrived,
            pltpu.VMEM((SLOTS, WIDTH), half),
            pltpu.VMEM((ORB, ORB, SLOTS), half),
            pltpu.VMEM((PB, 64, 64), jnp.float32),
            pltpu.VMEM((1024, 1024), half),
            pltpu.VMEM((256, 256), half),
            pltpu.VMEM((SLOTS, 2 * SLOTS), half),
            pltpu.VMEM((SLOTS, 2 * SLOTS), half),
            pltpu.VMEM((4, 1024, SLOTS), jnp.float32),
            pltpu.VMEM((ORB, ORB, SLOTS), half),
            pltpu.VMEM((SLOTS, SLOTS), jnp.float32),
            pltpu.VMEM((2 * MOST, MOST, 16, 128), half),
            pltpu.VMEM((PAIRS, MOST, 16, 128), half),
            pltpu.VMEM((PAIRS + 1, MOST, 16, 128), half),
            block,
            block,
            block,
            block,
            pltpu.SMEM((2, CAPS * PB), jnp.int32),
            dma((direct,)),
            dma,
            dma((direct, PAIRS)),
            dma((direct, PAIRS)),
            dma((2, STEPS, CHUNKS)),
            dma((2, STEPS, CHUNKS)),
            dma((PAIRS,)),
            dma((PAIRS,)),
            dma((TIMES,)),
            dma((TIMES,)),
            dma((TIMES,)),
            dma((TIMES,)),
        ],
        compiler_params=pltpu.CompilerParams(collective_id=0, has_side_effects=True),
        name="polarizability",
    )(
        pair_lists.T, cosine_weights, integrals.reshape(ROWS * CAPS, PB * WIDTH), coulomb_blocks,
        occ_density[0, 0], virt_density[0, 0],
    )


def solution(mesh):
    in_specs = (
        P("tensor", None, None),
        P(),
        P("tm", "tensor", None, None),
        P("tm", "tensor", None, None),
        P(),
        P(),
    )
    return jax.shard_map(
        per_device, mesh=mesh, in_specs=in_specs, out_specs=P("tm", "tensor", None), check_vma=False
    )
```

time: 455 us -> 93.9 us (0.21)
  waiting for transfers between devices: 204 us -> 0 us
  local copies, waits for them, and re-layouts: 152 us -> 1.57 us
  Pallas kernels: 0 us -> 91.8 us
  blocking collectives: 40.5 us -> 0 us
  matrix products: 19.6 us -> 0 us
  between operations: 13.6 us -> 0.01 us
  other arithmetic: 11.9 us -> 0 us
  starting transfers between devices: 10.5 us -> 0 us
    reduce_scatter x1 -> x0, waiting for transfers between devices: 107 us -> none  [per_device(): lax.psum_scatter(partial_value.astype(jnp.bfloat16), 'tensor', scatter_di...]
    all_to_all x1 -> x0, waiting for transfers between devices: 97.5 us -> none  [per_device(): lax.all_to_all(outgoing, 'tensor', split_axis=0, concat_axis=0, tiled=True)]
    pallas_call x0 -> x1, Pallas kernels: none -> 91.8 us  [per_device(): pl.pallas_call(kernel, out_shape=jax.ShapeDtypeStruct((1, ROWS, PB * 64),...]
    scatter x2 -> x0, local copies, waits for them, and re-layouts: 71.9 us -> none  [the longest x1 65.3 us: pack_rows(): filled = zero_buffer.at[targets, places].set(local_rows)]
    all_to_all x2 -> x0, blocking collectives: 40.5 us -> none  [the longest x1 25 us: per_device(): lax.all_to_all(chi_rows[None].astype(jnp.bfloat16), 'tm', split_axis=2, c...]
    convert_element_type x6 -> x0, local copies, waits for them, and re-layouts: 25.5 us -> none  [the longest x1 12.3 us: density_product(): contracted.astype(jnp.bfloat16)]
    dot_general x5 -> x0, matrix products: 19.6 us -> none  [the longest x1 6.78 us: density_product(): jnp.einsum('rms,ml->rls', half_done, occupied, preferred_element_type=jnp...]
    gather x2 -> x0, local copies, waits for them, and re-layouts: 13.3 us -> none  [the longest x1 12.7 us: per_device(): tile_rows = jnp.take(arrived, wanted, axis=0, mode='fill', fill_value=0)]
  transfers between devices with their start and end apart: 2 -> 0, of which waited for: 2 -> 0; matrix products, arithmetic and copies ran while one was open for 0% -> 0% of each run, Pallas kernels for 0% -> 0%
where the time goes in v2:
time: 93.9 us; the launch traced here: 93.4 us
  Pallas kernels  91.8 us (98%)
  local copies, waits for them, and re-layouts  1.57 us (2%)
    pallas_call x1, Pallas kernels, per_device(): pl.pallas_call(kernel, out_shape=jax.ShapeDtypeStruct((1, ROWS, PB * 64),...  91.8 us

profile of v2, /device:TPU:6, one launch (start us, length us, event | category | flops | bytes accessed | tf_op | source)
XLA Modules:
  0.0 93.4 jit_solution(9982443364805486160)
XLA Ops:
  0.0 91.8 %polarizability.1 = f32[1,32,1024]{2,1,0:T(8,128)} custom-call(s32[8,16]{1,0:T(8,128)} %bitcast.7, f32[16,16]{1,0:T(8,128)} %cos_ref.1, bf16[256,4096]{1,0:T(8,128)(2,1)} %bitcast.4, f32[16,64,64]{2,1,0:T(8,128)} %factor_ref.1, bf16[64,64]{1,0:T(8,128)(2,1)} %bitcast.5, bf16[64,64]{1,0:T(8,128)(2,1)} %bitcast.6), custom_call_target="tpu_custom_call" | custom-call | tf_op jit(solution)/shard_map/polarizability/pallas_call | solution.py:334
  91.9 1.6 %copy.8 = f32[1,32,1024]{2,1,0:T(8,128)} copy(f32[1,32,1024]{2,1,0:T(8,128)} %polarizability.1) | data formatting | bytes 262144

commit v3 on v2

v3 whole, which is shorter than its diff:
```python
import jax
import jax.numpy as jnp
from jax import lax
from jax.experimental import pallas as pl
from jax.experimental.pallas import tpu as pltpu
from jax.sharding import PartitionSpec as P

MESH = pl.DeviceIdType.MESH
MOST = 6
PB = 16
CAPS = 8
ORB = 64
ROWS = 32
PAIRS = 32
TIMES = 16
WIDTH = 256
SLOTS = MOST * 64
HALF = 128
STEPS = 6
NT = (((1,), (1,)), ((), ()))
TN = (((0,), (0,)), ((), ()))
ORDER = (0, 1, -1, 2, -2, 3, -3, 8, 4, -4, 7, 5, -5, -7, 6, -6)
PLACE = {distance: place for place, distance in enumerate(ORDER)}
DIRECT = (0, 8, 7, -7)


def iota(shape, axis):
    return lax.broadcasted_iota(jnp.int32, shape, axis)


def one_hot(mask):
    return mask.astype(jnp.float32).astype(jnp.bfloat16)


def mul(a, b, dims=None):
    if dims is None:
        return jnp.dot(a, b, preferred_element_type=jnp.float32)
    return lax.dot_general(a, b, dims, preferred_element_type=jnp.float32)


def low(x):
    return x.astype(jnp.bfloat16)


def kernel(
    lists_ref, cos_ref, rows_ref, factor_ref, occ_ref, virt_ref, out_ref,
    mine, route, early, stage, near0, near1, got1, got2, got3, tiles, factor, ko, kv, wide, part, half, mixed,
    gram, folded, terms, inbox, chi, times, spread, freqs, places,
    load_sem, factor_sem, send0, recv0, send1, recv1, sendz, recvz, send2, recv2, send3, recv3, send4, recv4,
):
    z = lax.axis_index("tm")
    me = lax.axis_index("tensor")
    got = (None, got1, got2, got3)
    near = (near0, near1)
    block = lax.div(me, 2)
    first = pl.multiple_of(lax.rem(me, 2) * ROWS, ROWS)

    def at(distance):
        return lax.rem(z + distance + TIMES, TIMES)

    def load(e):
        columns = pl.ds(pl.multiple_of(at(DIRECT[e]) * WIDTH, WIDTH), WIDTH)
        return pltpu.make_async_copy(rows_ref.at[:, columns], mine.at[e], load_sem.at[e])

    for e in range(len(DIRECT)):
        load(e).start()
    fetch = pltpu.make_async_copy(factor_ref, factor, factor_sem)
    fetch.start()

    barrier = pltpu.get_barrier_semaphore()

    def greet(i, carry):
        peer = lax.rem(me + i, PAIRS)
        pl.semaphore_signal(barrier, inc=1, device_id={"tensor": peer}, device_id_type=MESH)
        return carry

    for distance in (2, -2, 1, -1):
        pl.semaphore_signal(barrier, inc=1, device_id={"tm": at(distance)}, device_id_type=MESH)
    lax.fori_loop(1, PAIRS, greet, 0)

    column = lax.rem(iota((1, WIDTH), 1), CAPS)
    names = jnp.full((1, WIDTH), -1, jnp.int32)
    for c in range(CAPS):
        names = jnp.where(column == c, lists_ref[c, block], names)
    shape = (ROWS, WIDTH)
    code = jnp.where(iota(shape, 0) == jnp.right_shift(iota(shape, 1), 3), names, -1)
    for k in range(PAIRS):
        route[ROWS * k : ROWS * k + ROWS] = one_hot(code == k)

    def pack(e):
        load(e).wait()
        return low(mul(route[...], mine[e])).reshape(PAIRS, ROWS, WIDTH)

    packed = pack(0)
    for c in range(2):
        early[c] = packed[:, :, HALF * c : HALF * c + HALF]
    pl.semaphore_wait(barrier, PAIRS + 3)

    def exchange(e, i):
        peer = lax.rem(me + i, PAIRS)
        if e < 2:
            src, dst, send, recv = early.at[e, peer], near[e], send0.at[e, i], recv0.at[e, i]
        else:
            src, dst = stage.at[e - 2, peer], got[e - 1]
            send, recv = send1.at[e - 2, i], recv1.at[e - 2, i]
        return pltpu.make_async_remote_copy(
            src_ref=src,
            dst_ref=dst.at[block, pl.ds(first, ROWS)],
            send_sem=send,
            recv_sem=recv,
            device_id={"tensor": peer},
            device_id_type=MESH,
        )

    def send_rows(e):
        def start(i, carry):
            exchange(e, i).start()
            return carry

        lax.fori_loop(1, PAIRS, start, 0)

    send_rows(0)
    send_rows(1)

    members, ranks, count = [], [], jnp.int32(0)
    for p in range(PB):
        named = lists_ref[0, p] == me
        for c in range(1, CAPS):
            named = named | (lists_ref[c, p] == me)
        members.append(named)
        ranks.append(count)
        count = count + named.astype(jnp.int32)
    chosen = []
    for j in range(MOST):
        found = jnp.int32(PB)
        for p in range(PB):
            found = jnp.where(members[p] & (ranks[p] == j), p, found)
        chosen.append(found)
    slot_of = [jnp.where(members[p], jnp.minimum(ranks[p], MOST - 1), 0) for p in range(PB)]

    for c in range(2):
        near[c][PB] = jnp.zeros((64, HALF), jnp.bfloat16)
        near[c][block, pl.ds(first, ROWS)] = early[c, me]

    square = (ORB, ORB)
    held = jnp.right_shift(iota(square, 0), 2)
    owner = jnp.zeros(square, jnp.int32)
    for place, distance in enumerate(ORDER):
        owner = jnp.where(held == place, at(distance), owner)
    order = one_hot(iota(square, 1) == 4 * owner + jnp.bitwise_and(iota(square, 0), 3))
    occ = low(mul(low(mul(order, occ_ref[...])), order, NT))
    big = ORB * 16
    pick = one_hot(jnp.right_shift(iota((big, ORB), 0), 4) == iota((big, ORB), 1))
    full = mul(low(mul(pick, occ, NT)), pick, NT)
    same = jnp.bitwise_and(jnp.bitwise_xor(iota((big, big), 0), iota((big, big), 1)), 15) == 0
    ko[...] = low(jnp.where(same, full, 0.0))
    pick = one_hot(jnp.bitwise_and(iota((HALF, ORB), 0), ORB - 1) == iota((HALF, ORB), 1))
    full = mul(low(mul(pick, virt_ref[...], NT)), pick, NT)
    same = jnp.bitwise_xor(iota((HALF, HALF), 0), iota((HALF, HALF), 1)) < ORB
    kv[...] = low(jnp.where(same, full, 0.0))
    for e in range(1, len(DIRECT)):
        stage[e - 1] = pack(e)
        got[e][PB] = jnp.zeros((64, WIDTH), jnp.bfloat16)
        got[e][block, pl.ds(first, ROWS)] = stage[e - 1, me]

    def finish_rows(e):
        def finish(i, carry):
            exchange(e, i).wait()
            return carry

        lax.fori_loop(1, PAIRS, finish, 0)

    def take_half(c):
        finish_rows(c)
        for j in range(MOST):
            tiles[0, c, 64 * j : 64 * j + 64] = near[c][chosen[j]]

    def take_rows(e):
        finish_rows(e + 1)
        place = PLACE[DIRECT[e]]
        for j in range(MOST):
            rows = got[e][chosen[j]]
            for c in range(2):
                tiles[place, c, 64 * j : 64 * j + 64] = rows[:, HALF * c : HALF * c + HALF]
        virtual(place)

    def virtual(place):
        for c in range(2):
            value = low(mul(kv[...], tiles[place, c], NT)).reshape(2, ORB, SLOTS)
            half[4 * place + 2 * c : 4 * place + 2 * c + 2] = value

    def virtuals(distance):
        virtual(PLACE[distance])
        virtual(PLACE[-distance])

    def hop(way, step, chunk):
        sign = -1 if way == 0 else 1
        return pltpu.make_async_remote_copy(
            src_ref=tiles.at[PLACE[sign * (step - 1)], chunk],
            dst_ref=tiles.at[PLACE[sign * step], chunk],
            send_sem=sendz.at[way, step - 1, chunk],
            recv_sem=recvz.at[way, step - 1, chunk],
            device_id={"tm": at(-sign)},
            device_id_type=MESH,
        )

    def contract(b, g0, g1):
        def one(g, carry):
            nus = pl.ds(pl.multiple_of(g * 16, 16), 16)
            x = half[16 * b : 16 * b + 16, nus, :].reshape(WIDTH, SLOTS)
            y = mul(ko[:, WIDTH * b : WIDTH * b + WIDTH], x)
            if b == 0:
                part[g] = y
            elif b < 3:
                part[g] += y
            else:
                mixed[:, nus, :] = low(part[g] + y).reshape(ORB, 16, SLOTS)
            return carry

        lax.fori_loop(g0, g1, one, 0)

    def factors():
        fetch.wait()
        wide[...] = jnp.zeros_like(wide)
        shape = (ORB, 2 * ORB)
        ahead = one_hot(iota(shape, 0) == iota(shape, 1))
        behind = one_hot(iota(shape, 0) + ORB == iota(shape, 1))
        for j in range(MOST):
            value = low(factor[jnp.minimum(chosen[j], PB - 1)])
            m, n = j // 2, j % 2
            wide[m, 64 * n : 64 * n + 64, 128 * n : 128 * n + 128] = low(mul(value, ahead))
            lanes = slice(256 + 128 * n, 384 + 128 * n)
            wide[m, 64 * n : 64 * n + 64, lanes] = low(mul(value, behind))

    under = {
        (1, 0): (),
        (1, 1): (factors, lambda: virtual(0)),
        (2, 1): (lambda: virtuals(1),),
        (3, 1): (lambda: virtuals(2), lambda: contract(0, 0, 2)),
        (4, 0): (lambda: contract(0, 2, 4),),
        (4, 1): (lambda: virtuals(3), lambda: take_rows(1)),
        (5, 0): (lambda: contract(1, 0, 2),),
        (5, 1): (lambda: virtuals(4), lambda: contract(1, 2, 4)),
        (6, 0): (lambda: take_rows(2),),
        (6, 1): (lambda: virtuals(5), lambda: contract(2, 0, 4)),
    }
    for step in range(1, STEPS + 1):
        for chunk in range(2):
            if step == 1:
                take_half(chunk)
            for way in range(2):
                if step > 1:
                    hop(way, step - 1, chunk).wait_recv()
                hop(way, step, chunk).start()
            if step == 1 and chunk == 1:
                for e in range(1, len(DIRECT)):
                    send_rows(e + 1)
            for work in under.get((step, chunk), ()):
                work()
    take_rows(3)
    for chunk in range(2):
        for way in range(2):
            hop(way, STEPS, chunk).wait_recv()
    virtuals(STEPS)
    contract(3, 0, 4)
    gram[...] = jnp.zeros_like(gram)

    def overlap(b, carry):
        rows = jnp.concatenate([tiles[4 * b + i, c] for i in range(4) for c in range(2)], axis=1)
        gram[...] += mul(rows, mixed[pl.ds(16 * b, 16)].reshape(4 * WIDTH, SLOTS))
        return carry

    lax.fori_loop(0, 4, overlap, 0)
    term = low(jnp.transpose(gram[...]))
    for m in range(MOST // 2):
        value = mul(term[:, 128 * m : 128 * m + 128], wide[m])
        for b in range(2 * MOST):
            upper, lower = value[32 * b : 32 * b + 16], value[32 * b + 16 : 32 * b + 32]
            for n in range(2):
                lanes = slice(128 * n, 128 * n + 128)
                after = slice(256 + 128 * n, 384 + 128 * n)
                folded[b, 2 * m + n] = low(upper[:, lanes] + lower[:, after])
    for d in range(PAIRS):
        terms[d] = folded[slot_of[d // 2] * 2 + d % 2]

    def trade(axis, count, src, dst, send, recv):
        here = lax.axis_index(axis)

        def one(i):
            peer = lax.rem(here + i, count)
            return pltpu.make_async_remote_copy(
                src_ref=src.at[peer],
                dst_ref=dst.at[here],
                send_sem=send.at[i],
                recv_sem=recv.at[i],
                device_id={axis: peer},
                device_id_type=MESH,
            )

        def begin(i, carry):
            one(i).start()
            return carry

        def end(i, carry):
            one(i).wait()
            return carry

        lax.fori_loop(1, count, begin, 0)
        dst[here] = src[here]
        return lambda: lax.fori_loop(1, count, end, 0)

    arrive = trade("tensor", PAIRS, terms, inbox, send2, recv2)
    inbox[PAIRS, 0] = jnp.zeros((16, 128), jnp.bfloat16)

    def locate(c, carry):
        name = lists_ref[c, block]
        rank = jnp.int32(0)
        for q in range(PB):
            named = lists_ref[0, q] == name
            for other in range(1, CAPS):
                named = named | (lists_ref[other, q] == name)
            places[0, c * PB + q] = jnp.where(named, name, PAIRS)
            places[1, c * PB + q] = jnp.where(named, jnp.minimum(rank, MOST - 1), 0)
            rank = rank + named.astype(jnp.int32)
        return carry

    lax.fori_loop(0, CAPS, locate, 0)
    for step in range(1, STEPS + 1):
        for chunk in range(2):
            for way in range(2):
                hop(way, step, chunk).wait_send()
    arrive()
    for q in range(PB):
        total = inbox[places[0, q], places[1, q]].astype(jnp.float32)
        for c in range(1, CAPS):
            spot = c * PB + q
            total += inbox[places[0, spot], places[1, spot]].astype(jnp.float32)
        chi[q] = low(total)

    trade("tm", TIMES, chi, times, send3, recv3)()
    series = [times[t].astype(jnp.float32) for t in range(TIMES)]
    for f in range(TIMES):
        total = cos_ref[f, 0] * series[0]
        for t in range(1, TIMES):
            total += cos_ref[f, t] * series[t]
        spread[f] = low(total)
    trade("tm", TIMES, spread, freqs, send4, recv4)()

    out_ref[...] = freqs[...]


def unfold_kernel(freqs_ref, out_ref):
    first = iota((16, 128), 1) < 64
    for m in range(PB // 2):
        even = freqs_ref[2 * m].astype(jnp.float32)
        odd = freqs_ref[2 * m + 1].astype(jnp.float32)
        lanes = slice(128 * m, 128 * m + 128)
        out_ref[0, 0:16, lanes] = jnp.where(first, even, pltpu.roll(odd, 64, 1))
        out_ref[0, 16:32, lanes] = jnp.where(first, pltpu.roll(even, 64, 1), odd)


def per_device(integrals, pair_lists, occ_density, virt_density, cosine_weights, coulomb_blocks):
    smem = pl.BlockSpec(memory_space=pltpu.SMEM)
    vmem = pl.BlockSpec(memory_space=pltpu.VMEM)
    hbm = pl.BlockSpec(memory_space=pl.ANY)
    dma = pltpu.SemaphoreType.DMA
    half = jnp.bfloat16
    direct = len(DIRECT)
    block = pltpu.VMEM((PB, 16, 128), half)
    near = pltpu.VMEM((PB + 1, 64, HALF), half)
    arrived = pltpu.VMEM((PB + 1, 64, WIDTH), half)
    freqs = pl.pallas_call(
        kernel,
        out_shape=jax.ShapeDtypeStruct((PB, 16, 128), half),
        in_specs=[smem, smem, hbm, hbm, vmem, vmem],
        out_specs=vmem,
        scratch_shapes=[
            pltpu.VMEM((direct, ROWS * CAPS, WIDTH), half),
            pltpu.VMEM((PAIRS * ROWS, ROWS * CAPS), half),
            pltpu.VMEM((2, PAIRS, ROWS, HALF), half),
            pltpu.VMEM((direct - 1, PAIRS, ROWS, WIDTH), half),
            near,
            near,
            arrived,
            arrived,
            arrived,
            pltpu.VMEM((TIMES, 2, SLOTS, HALF), half),
            pltpu.VMEM((PB, 64, 64), jnp.float32),
            pltpu.VMEM((1024, 1024), half),
            pltpu.VMEM((HALF, HALF), half),
            pltpu.VMEM((MOST // 2, 128, 512), half),
            pltpu.VMEM((4, 1024, SLOTS), jnp.float32),
            pltpu.VMEM((ORB, ORB, SLOTS), half),
            pltpu.VMEM((ORB, ORB, SLOTS), half),
            pltpu.VMEM((SLOTS, SLOTS), jnp.float32),
            pltpu.VMEM((2 * MOST, MOST, 16, 128), half),
            pltpu.VMEM((PAIRS, MOST, 16, 128), half),
            pltpu.VMEM((PAIRS + 1, MOST, 16, 128), half),
            block,
            block,
            block,
            block,
            pltpu.SMEM((2, CAPS * PB), jnp.int32),
            dma((direct,)),
            dma,
            dma((2, PAIRS)),
            dma((2, PAIRS)),
            dma((direct - 1, PAIRS)),
            dma((direct - 1, PAIRS)),
            dma((2, STEPS, 2)),
            dma((2, STEPS, 2)),
            dma((PAIRS,)),
            dma((PAIRS,)),
            dma((TIMES,)),
            dma((TIMES,)),
            dma((TIMES,)),
            dma((TIMES,)),
        ],
        compiler_params=pltpu.CompilerParams(collective_id=0, has_side_effects=True),
        name="polarizability",
    )(
        pair_lists.T, cosine_weights, integrals.reshape(ROWS * CAPS, PB * WIDTH), coulomb_blocks,
        occ_density[0, 0], virt_density[0, 0],
    )
    return pl.pallas_call(
        unfold_kernel,
        out_shape=jax.ShapeDtypeStruct((1, ROWS, PB * 64), jnp.float32),
        in_specs=[vmem],
        out_specs=vmem,
        name="unfold",
    )(freqs)


def solution(mesh):
    in_specs = (
        P("tensor", None, None),
        P(),
        P("tm", "tensor", None, None),
        P("tm", "tensor", None, None),
        P(),
        P(),
    )
    return jax.shard_map(
        per_device, mesh=mesh, in_specs=in_specs, out_specs=P("tm", "tensor", None), check_vma=False
    )
```

time: 93.9 us -> 86.8 us (0.924)
  Pallas kernels: 91.8 us -> 86.3 us
  local copies, waits for them, and re-layouts: 1.57 us -> 0 us
    pallas_call x1 -> x2, Pallas kernels: 91.8 us -> 86.3 us  [the longest x1 84.7 us: per_device(): pl.pallas_call(kernel, out_shape=jax.ShapeDtypeStruct((PB, 16, 128), half...]
    unnamed x1 -> x0, local copies, waits for them, and re-layouts: 1.57 us -> none
where the time goes in v3:
time: 86.8 us; the launch traced here: 86.3 us
  Pallas kernels  86.3 us (99%)
    pallas_call x1, Pallas kernels, per_device(): pl.pallas_call(kernel, out_shape=jax.ShapeDtypeStruct((PB, 16, 128), half...  84.7 us

profile of v3, /device:TPU:6, one launch (start us, length us, event | category | flops | bytes accessed | tf_op | source)
XLA Modules:
  0.0 86.3 jit_solution(17350062327438642438)
XLA Ops:
  0.0 84.7 %polarizability.1.freqs_ref = bf16[16,16,128]{2,1,0:T(8,128)(2,1)} custom-call(s32[8,16]{1,0:T(8,128)} %bitcast.7, f32[16,16]{1,0:T(8,128)} %cos_ref.1, bf16[256,4096]{1,0:T(8,128)(2,1)} %bitcast.4, f32[16,64,64]{2,1,0:T(8,128)} %factor_ref.1, bf16[64,64]{1,0:T(8,128)(2,1)} %bitcast.5, bf16[64,64]{1,0:T(8,128)(2,1)} %bitcast.6), custom_call_target="tpu_custom_call" | custom-call | tf_op jit(solution)/shard_map/polarizability/pallas_call | solution.py:372
  84.8 1.6 %unfold.1 = f32[1,32,1024]{2,1,0:T(8,128)} custom-call(bf16[16,16,128]{2,1,0:T(8,128)(2,1)} %polarizability.1.freqs_ref), custom_call_target="tpu_custom_call" | custom-call | tf_op jit(solution)/shard_map/unfold/pallas_call | solution.py:425

commit v4 on v3

--- a/solution.py
+++ b/solution.py
@@ -45,7 +45,7 @@
 def kernel(
     lists_ref, cos_ref, rows_ref, factor_ref, occ_ref, virt_ref, out_ref,
     mine, route, early, stage, near0, near1, got1, got2, got3, tiles, factor, ko, kv, wide, part, half, mixed,
-    gram, folded, terms, inbox, chi, times, spread, freqs, places,
+    folded, terms, inbox, chi, times, spread, freqs, places,
     load_sem, factor_sem, send0, recv0, send1, recv1, sendz, recvz, send2, recv2, send3, recv3, send4, recv4,
 ):
     z = lax.axis_index("tm")
@@ -91,9 +91,12 @@
         load(e).wait()
         return low(mul(route[...], mine[e])).reshape(PAIRS, ROWS, WIDTH)
 
-    packed = pack(0)
-    for c in range(2):
-        early[c] = packed[:, :, HALF * c : HALF * c + HALF]
+    def pack_half(c):
+        part_rows = mine[0, :, HALF * c : HALF * c + HALF]
+        early[c] = low(mul(route[...], part_rows)).reshape(PAIRS, ROWS, HALF)
+
+    load(0).wait()
+    pack_half(0)
     pl.semaphore_wait(barrier, PAIRS + 3)
 
     def exchange(e, i):
@@ -120,6 +123,7 @@
         lax.fori_loop(1, PAIRS, start, 0)
 
     send_rows(0)
+    pack_half(1)
     send_rows(1)
 
     members, ranks, count = [], [], jnp.int32(0)
@@ -150,15 +154,20 @@
     order = one_hot(iota(square, 1) == 4 * owner + jnp.bitwise_and(iota(square, 0), 3))
     occ = low(mul(low(mul(order, occ_ref[...])), order, NT))
     big = ORB * 16
-    pick = one_hot(jnp.right_shift(iota((big, ORB), 0), 4) == iota((big, ORB), 1))
-    full = mul(low(mul(pick, occ, NT)), pick, NT)
-    same = jnp.bitwise_and(jnp.bitwise_xor(iota((big, big), 0), iota((big, big), 1)), 15) == 0
-    ko[...] = low(jnp.where(same, full, 0.0))
+
+    def spread_occ(b):
+        pick = one_hot(jnp.right_shift(iota((big, ORB), 0), 4) == iota((big, ORB), 1))
+        rows = low(mul(pick, occ, NT))
+        full = mul(rows, pick[WIDTH * b : WIDTH * b + WIDTH], NT)
+        shape = (big, WIDTH)
+        same = jnp.bitwise_and(jnp.bitwise_xor(iota(shape, 0), iota(shape, 1)), 15) == 0
+        ko[:, WIDTH * b : WIDTH * b + WIDTH] = low(jnp.where(same, full, 0.0))
+
     pick = one_hot(jnp.bitwise_and(iota((HALF, ORB), 0), ORB - 1) == iota((HALF, ORB), 1))
     full = mul(low(mul(pick, virt_ref[...], NT)), pick, NT)
     same = jnp.bitwise_xor(iota((HALF, HALF), 0), iota((HALF, HALF), 1)) < ORB
     kv[...] = low(jnp.where(same, full, 0.0))
-    for e in range(1, len(DIRECT)):
+    def prepare_rows(e):
         stage[e - 1] = pack(e)
         got[e][PB] = jnp.zeros((64, WIDTH), jnp.bfloat16)
         got[e][block, pl.ds(first, ROWS)] = stage[e - 1, me]
@@ -232,17 +241,27 @@
             lanes = slice(256 + 128 * n, 384 + 128 * n)
             wide[m, 64 * n : 64 * n + 64, lanes] = low(mul(value, behind))
 
+    def send_later(e):
+        prepare_rows(e)
+        send_rows(e + 1)
+
     under = {
-        (1, 0): (),
-        (1, 1): (factors, lambda: virtual(0)),
-        (2, 1): (lambda: virtuals(1),),
+        (1, 1): (
+            lambda: send_later(1),
+            lambda: send_later(2),
+            lambda: send_later(3),
+            lambda: virtual(0),
+        ),
+        (2, 0): (lambda: spread_occ(0),),
+        (2, 1): (lambda: virtuals(1), lambda: spread_occ(1)),
+        (3, 0): (factors,),
         (3, 1): (lambda: virtuals(2), lambda: contract(0, 0, 2)),
         (4, 0): (lambda: contract(0, 2, 4),),
         (4, 1): (lambda: virtuals(3), lambda: take_rows(1)),
         (5, 0): (lambda: contract(1, 0, 2),),
         (5, 1): (lambda: virtuals(4), lambda: contract(1, 2, 4)),
-        (6, 0): (lambda: take_rows(2),),
-        (6, 1): (lambda: virtuals(5), lambda: contract(2, 0, 4)),
+        (6, 0): (lambda: take_rows(2), lambda: spread_occ(2)),
+        (6, 1): (lambda: virtuals(5), lambda: contract(2, 0, 4), lambda: spread_occ(3)),
     }
     for step in range(1, STEPS + 1):
         for chunk in range(2):
@@ -252,9 +271,6 @@
                 if step > 1:
                     hop(way, step - 1, chunk).wait_recv()
                 hop(way, step, chunk).start()
-            if step == 1 and chunk == 1:
-                for e in range(1, len(DIRECT)):
-                    send_rows(e + 1)
             for work in under.get((step, chunk), ()):
                 work()
     take_rows(3)
@@ -263,15 +279,9 @@
             hop(way, STEPS, chunk).wait_recv()
     virtuals(STEPS)
     contract(3, 0, 4)
-    gram[...] = jnp.zeros_like(gram)
-
-    def overlap(b, carry):
-        rows = jnp.concatenate([tiles[4 * b + i, c] for i in range(4) for c in range(2)], axis=1)
-        gram[...] += mul(rows, mixed[pl.ds(16 * b, 16)].reshape(4 * WIDTH, SLOTS))
-        return carry
-
-    lax.fori_loop(0, 4, overlap, 0)
-    term = low(jnp.transpose(gram[...]))
+    rows = jnp.concatenate([tiles[i, c] for i in range(TIMES) for c in range(2)], axis=1)
+    gram = mul(rows, mixed[...].reshape(TIMES * WIDTH, SLOTS))
+    term = low(jnp.transpose(gram))
     for m in range(MOST // 2):
         value = mul(term[:, 128 * m : 128 * m + 128], wide[m])
         for b in range(2 * MOST):
@@ -392,7 +402,6 @@
             pltpu.VMEM((4, 1024, SLOTS), jnp.float32),
             pltpu.VMEM((ORB, ORB, SLOTS), half),
             pltpu.VMEM((ORB, ORB, SLOTS), half),
-            pltpu.VMEM((SLOTS, SLOTS), jnp.float32),
             pltpu.VMEM((2 * MOST, MOST, 16, 128), half),
             pltpu.VMEM((PAIRS, MOST, 16, 128), half),
             pltpu.VMEM((PAIRS + 1, MOST, 16, 128), half),

time: 86.8 us -> 86.7 us (level)
  no operation moved by 1% of the time
where the time goes in v4:
time: 86.7 us; the launch traced here: 86.3 us
  Pallas kernels  86.3 us (100%)
    pallas_call x1, Pallas kernels, per_device(): pl.pallas_call(kernel, out_shape=jax.ShapeDtypeStruct((PB, 16, 128), half...  84.8 us

profile of v4, /device:TPU:6, one launch (start us, length us, event | category | flops | bytes accessed | tf_op | source)
XLA Modules:
  0.0 86.3 jit_solution(13056761012603079434)
XLA Ops:
  0.0 84.8 %polarizability.1.freqs_ref = bf16[16,16,128]{2,1,0:T(8,128)(2,1)} custom-call(s32[8,16]{1,0:T(8,128)} %bitcast.7, f32[16,16]{1,0:T(8,128)} %cos_ref.1, bf16[256,4096]{1,0:T(8,128)(2,1)} %bitcast.4, f32[16,64,64]{2,1,0:T(8,128)} %factor_ref.1, bf16[64,64]{1,0:T(8,128)(2,1)} %bitcast.5, bf16[64,64]{1,0:T(8,128)(2,1)} %bitcast.6), custom_call_target="tpu_custom_call" | custom-call | tf_op jit(solution)/shard_map/polarizability/pallas_call | solution.py:382
  84.8 1.6 %unfold.1 = f32[1,32,1024]{2,1,0:T(8,128)} custom-call(bf16[16,16,128]{2,1,0:T(8,128)(2,1)} %polarizability.1.freqs_ref), custom_call_target="tpu_custom_call" | custom-call | tf_op jit(solution)/shard_map/unfold/pallas_call | solution.py:434

commit v5 on v4

--- a/solution.py
+++ b/solution.py
@@ -45,7 +45,7 @@
 def kernel(
     lists_ref, cos_ref, rows_ref, factor_ref, occ_ref, virt_ref, out_ref,
     mine, route, early, stage, near0, near1, got1, got2, got3, tiles, factor, ko, kv, wide, part, half, mixed,
-    folded, terms, inbox, chi, times, spread, freqs, places,
+    folded, terms, inbox, chi, times, spread, freqs, waves, places,
     load_sem, factor_sem, send0, recv0, send1, recv1, sendz, recvz, send2, recv2, send3, recv3, send4, recv4,
 ):
     z = lax.axis_index("tm")
@@ -245,6 +245,17 @@
         prepare_rows(e)
         send_rows(e + 1)
 
+    def cosines():
+        shape = (WIDTH, TIMES)
+        pick = one_hot(jnp.right_shift(iota(shape, 0), 4) == iota(shape, 1))
+        high = low(cos_ref[...])
+        rest = low(cos_ref[...] - high.astype(jnp.float32))
+        same = jnp.bitwise_xor(iota((WIDTH, WIDTH), 0), iota((WIDTH, WIDTH), 1))
+        same = jnp.bitwise_and(same, 15) == 0
+        for n, piece in enumerate((high, rest)):
+            full = mul(low(mul(pick, piece)), pick, NT)
+            waves[:, WIDTH * n : WIDTH * n + WIDTH] = low(jnp.where(same, full, 0.0))
+
     under = {
         (1, 1): (
             lambda: send_later(1),
@@ -254,7 +265,7 @@
         ),
         (2, 0): (lambda: spread_occ(0),),
         (2, 1): (lambda: virtuals(1), lambda: spread_occ(1)),
-        (3, 0): (factors,),
+        (3, 0): (factors, cosines),
         (3, 1): (lambda: virtuals(2), lambda: contract(0, 0, 2)),
         (4, 0): (lambda: contract(0, 2, 4),),
         (4, 1): (lambda: virtuals(3), lambda: take_rows(1)),
@@ -348,12 +359,9 @@
         chi[q] = low(total)
 
     trade("tm", TIMES, chi, times, send3, recv3)()
-    series = [times[t].astype(jnp.float32) for t in range(TIMES)]
-    for f in range(TIMES):
-        total = cos_ref[f, 0] * series[0]
-        for t in range(1, TIMES):
-            total += cos_ref[f, t] * series[t]
-        spread[f] = low(total)
+    series = times[...].reshape(TIMES * 16, 128)
+    total = mul(waves[:, :WIDTH], series) + mul(waves[:, WIDTH:], series)
+    spread[...] = low(total).reshape(TIMES, 16, 128)
     trade("tm", TIMES, spread, freqs, send4, recv4)()
 
     out_ref[...] = freqs[...]
@@ -382,7 +390,7 @@
     freqs = pl.pallas_call(
         kernel,
         out_shape=jax.ShapeDtypeStruct((PB, 16, 128), half),
-        in_specs=[smem, smem, hbm, hbm, vmem, vmem],
+        in_specs=[smem, vmem, hbm, hbm, vmem, vmem],
         out_specs=vmem,
         scratch_shapes=[
             pltpu.VMEM((direct, ROWS * CAPS, WIDTH), half),
@@ -409,6 +417,7 @@
             block,
             block,
             block,
+            pltpu.VMEM((WIDTH, 2 * WIDTH), half),
             pltpu.SMEM((2, CAPS * PB), jnp.int32),
             dma((direct,)),
             dma,

time: 86.7 us -> 86.6 us (level)
  no operation moved by 1% of the time
where the time goes in v5:
time: 86.6 us; the launch traced here: 86.3 us
  Pallas kernels  86.2 us (100%)
    pallas_call x1, Pallas kernels, per_device(): pl.pallas_call(kernel, out_shape=jax.ShapeDtypeStruct((PB, 16, 128), half...  84.7 us

profile of v5, /device:TPU:6, one launch (start us, length us, event | category | flops | bytes accessed | tf_op | source)
XLA Modules:
  0.0 86.3 jit_solution(17788320900876994928)
XLA Ops:
  0.0 84.7 %polarizability.1.freqs_ref = bf16[16,16,128]{2,1,0:T(8,128)(2,1)} custom-call(s32[8,16]{1,0:T(8,128)} %bitcast.7, f32[16,16]{1,0:T(8,128)} %cos_ref.1, bf16[256,4096]{1,0:T(8,128)(2,1)} %bitcast.4, f32[16,64,64]{2,1,0:T(8,128)} %factor_ref.1, bf16[64,64]{1,0:T(8,128)(2,1)} %bitcast.5, bf16[64,64]{1,0:T(8,128)(2,1)} %bitcast.6), custom_call_target="tpu_custom_call" | custom-call | tf_op jit(solution)/shard_map/polarizability/pallas_call | solution.py:390
  84.7 1.6 %unfold.1 = f32[1,32,1024]{2,1,0:T(8,128)} custom-call(bf16[16,16,128]{2,1,0:T(8,128)(2,1)} %polarizability.1.freqs_ref), custom_call_target="tpu_custom_call" | custom-call | tf_op jit(solution)/shard_map/unfold/pallas_call | solution.py:443
